TPU v7x, 32 devices: a whole 2x2x4 slice. The times are simulated.
32 devices in a mesh: tile: 8 (over z, x), wave: 4 (over y, core).
Axes of the slice: x: 2, y: 2, z: 4, core: 2. Of those that a mesh axis runs over, the one named last changes fastest.
Arguments:
- fibre_data: bfloat16 [128, 256, 128], P('wave', 'tile'), may hold values from -162 to 162
- kernels: bfloat16 [4, 256, 4, 128, 128], P('wave', 'tile'), may hold values from -0.25 to 0.25
- block_index: int32 [4, 256, 4], P('wave', 'tile'), may hold values from 0 to 127, as said below
- live_count: int32 [8], P('tile'), may hold values from 8 to 32, as said below
Outputs:
- solution: float32 [128, 128, 128], P('wave', 'tile')
- residual: float32 [128, 128, 128], P('wave', 'tile')
Inputs may be any that keep to these rules, and one draw needn't show every extreme that they name: `block_index`: A group of tile t (groups t * 32 to (t + 1) * 32 - 1) names only blocks from max(t * 16 - 4, 0) to min((t + 1) * 16 + 4, 128) - 1; for every kernel set and tile, some live group of that tile names both ends of that range. `live_count`: some tile has all 32 groups live.
All inputs are finite; a program needn't handle non-finite values.
Results may differ from a plain program's by a relative error of at most 0.035.
Values may be sent and summed in bfloat16 or wider, within the bound.
No kernel may reach another device: no remote copies, remote signals or barrier semaphores. Data moves between devices by JAX's collectives and lax.ppermute only.
A program may use at most 64 MiB of HBM per device.

v0:
```python
import jax
import jax.numpy as jnp
from jax import lax
from jax.sharding import PartitionSpec as P

HALO_BLOCKS = 4
BLOCKS_DEV = 16
ITERATIONS = 3
TIKHONOV = 0.5


def from_behind(value, axis, by):
    size = lax.axis_size(axis)
    pairs = [(i, i + by) for i in range(size) if 0 <= i + by < size]
    return lax.ppermute(value, axis, pairs)


def extended(value, sides, width):
    for axis, dim in sides:
        size, length = (lax.axis_size(axis), value.shape[dim])
        up = [(i, (i + 1) % size) for i in range(size - 1)]
        down = [(j, i) for i, j in up]
        last = lax.slice_in_dim(value, length - width, length, axis=dim)
        initial = lax.slice_in_dim(value, 0, width, axis=dim)
        before = lax.ppermute(last, axis, up)
        after = lax.ppermute(initial, axis, down)
        value = jnp.concatenate([before, value, after], axis=dim)
    return value


def select_table(local_index, extent):
    return (local_index[..., None] == jnp.arange(extent, dtype=jnp.int32)).astype(jnp.bfloat16)


def forward_image(window16, kernels, selector16, live_mask):
    kernel_sets = kernels.shape[0]
    shaped = window16.reshape(
        kernel_sets, window16.shape[0] // kernel_sets, window16.shape[1], window16.shape[2]
    )
    picked = jnp.einsum(
        "cgrb,cwbs->cwgrs", selector16, shaped, preferred_element_type=jnp.float32
    ).astype(jnp.bfloat16)
    applied = jnp.einsum("cwgrs,cgrsf->cwgf", picked, kernels, preferred_element_type=jnp.float32)
    return (applied * live_mask[None, None, :, None]).astype(jnp.bfloat16)


def adjoint_image(image16, kernels, selector16):
    spread = jnp.einsum("cwgf,cgrsf->cwgrs", image16, kernels, preferred_element_type=jnp.float32)
    upper_part = spread.astype(jnp.bfloat16)
    lower_part = (spread - upper_part.astype(jnp.float32)).astype(jnp.bfloat16)
    summed = jnp.einsum(
        "cgrb,cwgrs->cwbs", selector16, upper_part, preferred_element_type=jnp.float32
    )
    summed = summed + jnp.einsum(
        "cgrb,cwgrs->cwbs", selector16, lower_part, preferred_element_type=jnp.float32
    )
    return summed.reshape(summed.shape[0] * summed.shape[1], summed.shape[2], summed.shape[3])


def shards(fibre_data, kernels, block_index, live_count):
    extent = BLOCKS_DEV + 2 * HALO_BLOCKS
    first_block = lax.axis_index("tile") * BLOCKS_DEV - HALO_BLOCKS
    selector16 = select_table(block_index - first_block, extent)
    groups = block_index.shape[1]
    live_mask = (jnp.arange(groups, dtype=jnp.int32) < live_count[0]).astype(jnp.float32)
    kernel_sets = kernels.shape[0]
    observed = fibre_data * live_mask.astype(jnp.bfloat16)[None, :, None]
    observed = observed.reshape(
        kernel_sets, fibre_data.shape[0] // kernel_sets, groups, fibre_data.shape[2]
    )
    partial_rhs = adjoint_image(observed, kernels, selector16)
    rim_width = HALO_BLOCKS

    def settle(partial_value):
        owned_part = partial_value[:, rim_width : rim_width + BLOCKS_DEV]
        from_right = from_behind(
            partial_value[:, :rim_width].astype(jnp.bfloat16), "tile", -1
        ).astype(jnp.float32)
        from_left = from_behind(
            partial_value[:, BLOCKS_DEV + rim_width :].astype(jnp.bfloat16), "tile", 1
        ).astype(jnp.float32)
        owned_part = owned_part.at[:, :rim_width].add(from_left)
        return owned_part.at[:, BLOCKS_DEV - rim_width :].add(from_right)

    def operate(vector):
        padded = extended(vector.astype(jnp.bfloat16), (("tile", 1),), HALO_BLOCKS)
        image16 = forward_image(padded, kernels, selector16, live_mask)
        return settle(adjoint_image(image16, kernels, selector16)) + TIKHONOV * vector

    def local_inner(first_vector, second_vector):
        return jnp.sum(first_vector * second_vector)

    rhs = settle(partial_rhs)
    solution = jnp.zeros_like(rhs)
    residual = rhs

    def paired(vector, applied):
        return lax.psum(
            (local_inner(vector, vector), local_inner(vector, applied)), ("tile", "wave")
        )

    applied = operate(residual)
    current, product = paired(residual, applied)
    step_size = current / product
    direction = residual
    applied_dir = applied
    for iteration in range(ITERATIONS):
        solution = solution + step_size * direction
        residual = residual - step_size * applied_dir
        if iteration + 1 < ITERATIONS:
            applied = operate(residual)
            following, product = paired(residual, applied)
            beta_ratio = following / current
            step_size = following / (product - beta_ratio * following / step_size)
            direction = residual + beta_ratio * direction
            applied_dir = applied + beta_ratio * applied_dir
            current = following
    return (solution, residual)


def solution(mesh):
    in_specs = (
        P("wave", "tile", None),
        P("wave", "tile", None, None, None),
        P("wave", "tile", None),
        P("tile"),
    )
    out_specs = (P("wave", "tile", None), P("wave", "tile", None))
    return jax.shard_map(shards, mesh=mesh, in_specs=in_specs, out_specs=out_specs, check_vma=False)
```

profile of v0, /device:TPU:0, one launch (start us, length us, event | category | flops | bytes accessed | tf_op | source)
XLA Modules:
  0.0 242.5 jit_solution(4463199943497567733)
XLA Ops:
  2.3 3.7 %fusion.12 = f32[32,32,4,128]{3,1,2,0:T(8,128)S(1)} fusion(bf16[1,32,4,128,128]{4,3,2,1,0:T(8,128)(2,1)} %param.21, bf16[32,32,128,1]{2,1,0,3:T(8,128)(2,1)S(1)} %multiply_bitcast_fusion), kind=kOutput, calls=%fused_computation.12 | convolution fusion | flops 134217728 | bytes 6553600 | tf_op jit(solution)/shard_map/cwgf,cgrsf->cwgrs/dot_general | solution.py:48
  8.4 4.9 %collective-permute-start = (bf16[32,4,128]{2,1,0:T(4,128)(2,1)S(1)}, bf16[32,4,128]{2,1,0:T(4,128)(2,1)S(1)}, u32[]{:S(2)}, u32[]{:S(2)}) collective-permute-start(bf16[32,4,128]{2,1,0:T(4,128)(2,1)S(1)} %get-tuple-element.124), channel_id=1, source_target_pairs={{0,4},{4,8},{8,12},{12,16},{16,20},{20,24},{24,28},{1,5},{5,9},{9,... | collective-permute-start | bytes 98312 | tf_op jit(solution)/shard_map/ppermute | solution.py:15
  13.3 1.3 collective-permute-start.1
  14.9 4.2 %collective-permute-done.1 = bf16[32,4,128]{2,1,0:T(4,128)(2,1)S(1)} collective-permute-done((bf16[32,4,128]{2,1,0:T(4,128)(2,1)S(1)}, bf16[32,4,128]{2,1,0:T(4,128)(2,1)S(1)}, u32[]{:S(2)}, u32[]{:S(2)}) %collective-permute-start.1) | collective-permute-done | bytes 32800 | tf_op jit(solution)/shard_map/ppermute | solution.py:15
  19.2 1.3 collective-permute-start.3
  20.5 5.0 %collective-permute-start.2 = (bf16[32,4,128]{2,1,0:T(4,128)(2,1)S(1)}, bf16[32,4,128]{2,1,0:T(4,128)(2,1)S(1)}, u32[]{:S(2)}, u32[]{:S(2)}) collective-permute-start(bf16[32,4,128]{2,1,0:T(4,128)(2,1)S(1)} %get-tuple-element.129), channel_id=1, source_target_pairs={{0,4},{4,8},{8,12},{12,16},{16,20},{20,24},{24,28},{1,5},{5,9},{9,... | collective-permute-start | bytes 98312 | tf_op jit(solution)/shard_map/ppermute | solution.py:25
  25.6 1.6 collective-permute-done.2
  27.6 6.0 %fusion.8 = f32[32,32,4,128]{3,1,2,0:T(8,128)S(1)} fusion(bf16[1,32,4,128,128]{4,3,2,1,0:T(8,128)(2,1)} %param.21, bf16[32,32,4,128]{3,1,2,0:T(8,128)(2,1)S(1)} %fusion.18, f32[32]{0:T(128)S(1)} %compare_convert_fusion), kind=kOutput, calls=%fused_computation.8 | convolution fusion | flops 268697600 | bytes 7340160 | tf_op jit(solution)/shard_map/cwgf,cgrsf->cwgrs/dot_general | solution.py:48
  35.6 4.8 %collective-permute-start.4 = (bf16[32,4,128]{2,1,0:T(4,128)(2,1)S(1)}, bf16[32,4,128]{2,1,0:T(4,128)(2,1)S(1)}, u32[]{:S(2)}, u32[]{:S(2)}) collective-permute-start(bf16[32,4,128]{2,1,0:T(4,128)(2,1)S(1)} %get-tuple-element.122), channel_id=1, source_target_pairs={{0,4},{4,8},{8,12},{12,16},{16,20},{20,24},{24,28},{1,5},{5,9},{9,... | collective-permute-start | bytes 98312 | tf_op jit(solution)/shard_map/ppermute | solution.py:15
  42.0 5.4 %collective-permute-done.5 = bf16[32,4,128]{2,1,0:T(4,128)(2,1)S(1)} collective-permute-done((bf16[32,4,128]{2,1,0:T(4,128)(2,1)S(1)}, bf16[32,4,128]{2,1,0:T(4,128)(2,1)S(1)}, u32[]{:S(2)}, u32[]{:S(2)}) %collective-permute-start.5) | collective-permute-done | bytes 32800 | tf_op jit(solution)/shard_map/ppermute | solution.py:15
  48.2 42.1 %all-reduce.2 = (f32[]{:T(128)}, f32[]{:T(128)}) all-reduce(f32[]{:T(128)} %get-tuple-element.103, f32[]{:T(128)} %get-tuple-element.102), channel_id=1, replica_groups=mesh['tile'=8,'wave'=4] {'tile','wave'}, use_global_device_ids=true, to_apply=%region_1.0 | all-reduce | flops 2 | bytes 16 | tf_op jit(solution)/shard_map/psum | solution.py:98
  93.0 5.0 %collective-permute-start.6 = (bf16[32,4,128]{2,1,0:T(4,128)(2,1)S(1)}, bf16[32,4,128]{2,1,0:T(4,128)(2,1)S(1)}, u32[]{:S(2)}, u32[]{:S(2)}) collective-permute-start(bf16[32,4,128]{2,1,0:T(4,128)(2,1)S(1)} %get-tuple-element.127), channel_id=1, source_target_pairs={{0,4},{4,8},{8,12},{12,16},{16,20},{20,24},{24,28},{1,5},{5,9},{9,... | collective-permute-start | bytes 98312 | tf_op jit(solution)/shard_map/ppermute | solution.py:25
  98.0 1.4 collective-permute-done.6
  99.4 1.5 fusion.19
  100.8 6.3 %fusion.4 = f32[32,32,4,128]{3,1,2,0:T(8,128)S(1)} fusion(bf16[1,32,4,128,128]{4,3,2,1,0:T(8,128)(2,1)} %param.21, bf16[32,32,4,128]{3,1,2,0:T(8,128)(2,1)} %fusion.19, f32[32]{0:T(128)S(1)} %compare_convert_fusion), kind=kOutput, calls=%fused_computation.4 | convolution fusion | flops 268697600 | bytes 7340160 | tf_op jit(solution)/shard_map/cwgf,cgrsf->cwgrs/dot_general | solution.py:48
  109.1 4.8 %collective-permute-start.8 = (bf16[32,4,128]{2,1,0:T(4,128)(2,1)S(1)}, bf16[32,4,128]{2,1,0:T(4,128)(2,1)S(1)}, u32[]{:S(2)}, u32[]{:S(2)}) collective-permute-start(bf16[32,4,128]{2,1,0:T(4,128)(2,1)S(1)} %get-tuple-element.120), channel_id=1, source_target_pairs={{0,4},{4,8},{8,12},{12,16},{16,20},{20,24},{24,28},{1,5},{5,9},{9,... | collective-permute-start | bytes 98312 | tf_op jit(solution)/shard_map/ppermute | solution.py:15
  115.5 5.4 %collective-permute-done.9 = bf16[32,4,128]{2,1,0:T(4,128)(2,1)S(1)} collective-permute-done((bf16[32,4,128]{2,1,0:T(4,128)(2,1)S(1)}, bf16[32,4,128]{2,1,0:T(4,128)(2,1)S(1)}, u32[]{:S(2)}, u32[]{:S(2)}) %collective-permute-start.9) | collective-permute-done | bytes 32800 | tf_op jit(solution)/shard_map/ppermute | solution.py:15
  121.7 39.7 %all-reduce.1 = (f32[]{:T(128)}, f32[]{:T(128)}) all-reduce(f32[]{:T(128)} %get-tuple-element.101, f32[]{:T(128)} %get-tuple-element.100), channel_id=1, replica_groups=mesh['tile'=8,'wave'=4] {'tile','wave'}, use_global_device_ids=true, to_apply=%region_5.0 | all-reduce | flops 2 | bytes 16 | tf_op jit(solution)/shard_map/psum | solution.py:98
  168.2 4.8 %collective-permute-start.10 = (bf16[32,4,128]{2,1,0:T(4,128)(2,1)S(1)}, bf16[32,4,128]{2,1,0:T(4,128)(2,1)S(1)}, u32[]{:S(2)}, u32[]{:S(2)}) collective-permute-start(bf16[32,4,128]{2,1,0:T(4,128)(2,1)S(1)} %get-tuple-element.125), channel_id=1, source_target_pairs={{0,4},{4,8},{8,12},{12,16},{16,20},{20,24},{24,28},{1,5},{5,9},{9,... | collective-permute-start | bytes 98312 | tf_op jit(solution)/shard_map/ppermute | solution.py:25
  173.0 1.6 collective-permute-done.10
  175.1 6.0 %fusion = f32[32,32,4,128]{3,1,2,0:T(8,128)S(1)} fusion(bf16[1,32,4,128,128]{4,3,2,1,0:T(8,128)(2,1)} %param.21, bf16[32,32,4,128]{3,1,2,0:T(8,128)(2,1)S(1)} %fusion.20, f32[32]{0:T(128)S(1)} %compare_convert_fusion), kind=kOutput, calls=%fused_computation | convolution fusion | flops 268697600 | bytes 7340160 | tf_op jit(solution)/shard_map/cwgf,cgrsf->cwgrs/dot_general | solution.py:48
  183.1 4.8 %collective-permute-start.12 = (bf16[32,4,128]{2,1,0:T(4,128)(2,1)S(1)}, bf16[32,4,128]{2,1,0:T(4,128)(2,1)S(1)}, u32[]{:S(2)}, u32[]{:S(2)}) collective-permute-start(bf16[32,4,128]{2,1,0:T(4,128)(2,1)S(1)} %get-tuple-element.118), channel_id=1, source_target_pairs={{0,4},{4,8},{8,12},{12,16},{16,20},{20,24},{24,28},{1,5},{5,9},{9,... | collective-permute-start | bytes 98312 | tf_op jit(solution)/shard_map/ppermute | solution.py:15
  189.5 5.4 %collective-permute-done.13 = bf16[32,4,128]{2,1,0:T(4,128)(2,1)S(1)} collective-permute-done((bf16[32,4,128]{2,1,0:T(4,128)(2,1)S(1)}, bf16[32,4,128]{2,1,0:T(4,128)(2,1)S(1)}, u32[]{:S(2)}, u32[]{:S(2)}) %collective-permute-start.13) | collective-permute-done | bytes 32800 | tf_op jit(solution)/shard_map/ppermute | solution.py:15
  195.7 42.1 %all-reduce = (f32[]{:T(128)}, f32[]{:T(128)}) all-reduce(f32[]{:T(128)} %get-tuple-element.99, f32[]{:T(128)} %get-tuple-element.98), channel_id=1, replica_groups=mesh['tile'=8,'wave'=4] {'tile','wave'}, use_global_device_ids=true, to_apply=%region_9.0 | all-reduce | flops 2 | bytes 16 | tf_op jit(solution)/shard_map/psum | solution.py:98
  (70 shorter events, 22.0 us)
Async XLA Ops:
  6.4 0.7 copy-start.4
  8.4 6.5 %collective-permute-start = (bf16[32,4,128]{2,1,0:T(4,128)(2,1)S(1)}, bf16[32,4,128]{2,1,0:T(4,128)(2,1)S(1)}, u32[]{:S(2)}, u32[]{:S(2)}) collective-permute-start(bf16[32,4,128]{2,1,0:T(4,128)(2,1)S(1)} %get-tuple-element.124), channel_id=1, source_target_pairs={{0,4},{4,8},{8,12},{12,16},{16,20},{20,24},{24,28},{1,5},{5,9},{9,... | collective-permute-start | bytes 98312 | tf_op jit(solution)/shard_map/ppermute | solution.py:15
  13.3 5.8 %collective-permute-start.1 = (bf16[32,4,128]{2,1,0:T(4,128)(2,1)S(1)}, bf16[32,4,128]{2,1,0:T(4,128)(2,1)S(1)}, u32[]{:S(2)}, u32[]{:S(2)}) collective-permute-start(bf16[32,4,128]{2,1,0:T(4,128)(2,1)S(1)} %get-tuple-element.123), channel_id=1, source_target_pairs={{4,0},{8,4},{12,8},{16,12},{20,16},{24,20},{28,24},{5,1},{9,5},{13... | collective-permute-start | bytes 98312 | tf_op jit(solution)/shard_map/ppermute | solution.py:15
  19.2 6.3 %collective-permute-start.3 = (bf16[32,4,128]{2,1,0:T(4,128)(2,1)S(1)}, bf16[32,4,128]{2,1,0:T(4,128)(2,1)S(1)}, u32[]{:S(2)}, u32[]{:S(2)}) collective-permute-start(bf16[32,4,128]{2,1,0:T(4,128)(2,1)S(1)} %get-tuple-element.130), channel_id=1, source_target_pairs={{4,0},{8,4},{12,8},{16,12},{20,16},{24,20},{28,24},{5,1},{9,5},{13... | collective-permute-start | bytes 98312 | tf_op jit(solution)/shard_map/ppermute | solution.py:26
  20.5 6.6 %collective-permute-start.2 = (bf16[32,4,128]{2,1,0:T(4,128)(2,1)S(1)}, bf16[32,4,128]{2,1,0:T(4,128)(2,1)S(1)}, u32[]{:S(2)}, u32[]{:S(2)}) collective-permute-start(bf16[32,4,128]{2,1,0:T(4,128)(2,1)S(1)} %get-tuple-element.129), channel_id=1, source_target_pairs={{0,4},{4,8},{8,12},{12,16},{16,20},{20,24},{24,28},{1,5},{5,9},{9,... | collective-permute-start | bytes 98312 | tf_op jit(solution)/shard_map/ppermute | solution.py:25
  35.6 6.4 %collective-permute-start.4 = (bf16[32,4,128]{2,1,0:T(4,128)(2,1)S(1)}, bf16[32,4,128]{2,1,0:T(4,128)(2,1)S(1)}, u32[]{:S(2)}, u32[]{:S(2)}) collective-permute-start(bf16[32,4,128]{2,1,0:T(4,128)(2,1)S(1)} %get-tuple-element.122), channel_id=1, source_target_pairs={{0,4},{4,8},{8,12},{12,16},{16,20},{20,24},{24,28},{1,5},{5,9},{9,... | collective-permute-start | bytes 98312 | tf_op jit(solution)/shard_map/ppermute | solution.py:15
  40.4 7.0 %collective-permute-start.5 = (bf16[32,4,128]{2,1,0:T(4,128)(2,1)S(1)}, bf16[32,4,128]{2,1,0:T(4,128)(2,1)S(1)}, u32[]{:S(2)}, u32[]{:S(2)}) collective-permute-start(bf16[32,4,128]{2,1,0:T(4,128)(2,1)S(1)} %get-tuple-element.121), channel_id=1, source_target_pairs={{4,0},{8,4},{12,8},{16,12},{20,16},{24,20},{28,24},{5,1},{9,5},{13... | collective-permute-start | bytes 98312 | tf_op jit(solution)/shard_map/ppermute | solution.py:15
  91.7 74.3 %copy-start = (f32[32,16,128]{2,1,0:T(8,128)}, f32[32,16,128]{2,1,0:T(8,128)S(1)}, u32[]{:S(2)}) copy-start(f32[32,16,128]{2,1,0:T(8,128)S(1)} %get-tuple-element.114) | copy-start | bytes 786436
  91.7 6.3 %collective-permute-start.7 = (bf16[32,4,128]{2,1,0:T(4,128)(2,1)S(1)}, bf16[32,4,128]{2,1,0:T(4,128)(2,1)S(1)}, u32[]{:S(2)}, u32[]{:S(2)}) collective-permute-start(bf16[32,4,128]{2,1,0:T(4,128)(2,1)S(1)} %get-tuple-element.128), channel_id=1, source_target_pairs={{4,0},{8,4},{12,8},{16,12},{20,16},{24,20},{28,24},{5,1},{9,5},{13... | collective-permute-start | bytes 98312 | tf_op jit(solution)/shard_map/ppermute | solution.py:26
  93.0 6.4 %collective-permute-start.6 = (bf16[32,4,128]{2,1,0:T(4,128)(2,1)S(1)}, bf16[32,4,128]{2,1,0:T(4,128)(2,1)S(1)}, u32[]{:S(2)}, u32[]{:S(2)}) collective-permute-start(bf16[32,4,128]{2,1,0:T(4,128)(2,1)S(1)} %get-tuple-element.127), channel_id=1, source_target_pairs={{0,4},{4,8},{8,12},{12,16},{16,20},{20,24},{24,28},{1,5},{5,9},{9,... | collective-permute-start | bytes 98312 | tf_op jit(solution)/shard_map/ppermute | solution.py:25
  109.1 6.4 %collective-permute-start.8 = (bf16[32,4,128]{2,1,0:T(4,128)(2,1)S(1)}, bf16[32,4,128]{2,1,0:T(4,128)(2,1)S(1)}, u32[]{:S(2)}, u32[]{:S(2)}) collective-permute-start(bf16[32,4,128]{2,1,0:T(4,128)(2,1)S(1)} %get-tuple-element.120), channel_id=1, source_target_pairs={{0,4},{4,8},{8,12},{12,16},{16,20},{20,24},{24,28},{1,5},{5,9},{9,... | collective-permute-start | bytes 98312 | tf_op jit(solution)/shard_map/ppermute | solution.py:15
  113.9 7.0 %collective-permute-start.9 = (bf16[32,4,128]{2,1,0:T(4,128)(2,1)S(1)}, bf16[32,4,128]{2,1,0:T(4,128)(2,1)S(1)}, u32[]{:S(2)}, u32[]{:S(2)}) collective-permute-start(bf16[32,4,128]{2,1,0:T(4,128)(2,1)S(1)} %get-tuple-element.119), channel_id=1, source_target_pairs={{4,0},{8,4},{12,8},{16,12},{20,16},{24,20},{28,24},{5,1},{9,5},{13... | collective-permute-start | bytes 98312 | tf_op jit(solution)/shard_map/ppermute | solution.py:15
  166.9 6.1 %collective-permute-start.11 = (bf16[32,4,128]{2,1,0:T(4,128)(2,1)S(1)}, bf16[32,4,128]{2,1,0:T(4,128)(2,1)S(1)}, u32[]{:S(2)}, u32[]{:S(2)}) collective-permute-start(bf16[32,4,128]{2,1,0:T(4,128)(2,1)S(1)} %get-tuple-element.126), channel_id=1, source_target_pairs={{4,0},{8,4},{12,8},{16,12},{20,16},{24,20},{28,24},{5,1},{9,5},{13... | collective-permute-start | bytes 98312 | tf_op jit(solution)/shard_map/ppermute | solution.py:26
  168.2 6.4 %collective-permute-start.10 = (bf16[32,4,128]{2,1,0:T(4,128)(2,1)S(1)}, bf16[32,4,128]{2,1,0:T(4,128)(2,1)S(1)}, u32[]{:S(2)}, u32[]{:S(2)}) collective-permute-start(bf16[32,4,128]{2,1,0:T(4,128)(2,1)S(1)} %get-tuple-element.125), channel_id=1, source_target_pairs={{0,4},{4,8},{8,12},{12,16},{16,20},{20,24},{24,28},{1,5},{5,9},{9,... | collective-permute-start | bytes 98312 | tf_op jit(solution)/shard_map/ppermute | solution.py:25
  181.7 13.3 %copy-start.2 = (f32[32,16,128]{2,1,0:T(8,128)S(1)}, f32[32,16,128]{2,1,0:T(8,128)}, u32[]{:S(2)}) copy-start(f32[32,16,128]{2,1,0:T(8,128)} %get-tuple-element.111) | copy-start | bytes 786436
  182.3 59.2 %copy-start.1 = (f32[32,16,128]{2,1,0:T(8,128)S(1)}, f32[32,16,128]{2,1,0:T(8,128)}, u32[]{:S(2)}) copy-start(f32[32,16,128]{2,1,0:T(8,128)} %copy-done) | copy-start | bytes 786436
  182.3 59.2 %copy-start.3 = (f32[32,16,128]{2,1,0:T(8,128)S(1)}, f32[32,16,128]{2,1,0:T(8,128)}, u32[]{:S(2)}) copy-start(f32[32,16,128]{2,1,0:T(8,128)} %get-tuple-element.112) | copy-start | bytes 786436
  183.1 6.4 %collective-permute-start.12 = (bf16[32,4,128]{2,1,0:T(4,128)(2,1)S(1)}, bf16[32,4,128]{2,1,0:T(4,128)(2,1)S(1)}, u32[]{:S(2)}, u32[]{:S(2)}) collective-permute-start(bf16[32,4,128]{2,1,0:T(4,128)(2,1)S(1)} %get-tuple-element.118), channel_id=1, source_target_pairs={{0,4},{4,8},{8,12},{12,16},{16,20},{20,24},{24,28},{1,5},{5,9},{9,... | collective-permute-start | bytes 98312 | tf_op jit(solution)/shard_map/ppermute | solution.py:15
  187.9 7.0 %collective-permute-start.13 = (bf16[32,4,128]{2,1,0:T(4,128)(2,1)S(1)}, bf16[32,4,128]{2,1,0:T(4,128)(2,1)S(1)}, u32[]{:S(2)}, u32[]{:S(2)}) collective-permute-start(bf16[32,4,128]{2,1,0:T(4,128)(2,1)S(1)} %get-tuple-element.117), channel_id=1, source_target_pairs={{4,0},{8,4},{12,8},{16,12},{20,16},{24,20},{28,24},{5,1},{9,5},{13... | collective-permute-start | bytes 98312 | tf_op jit(solution)/shard_map/ppermute | solution.py:15
where the time goes:
time: 244 us; the launch traced here: 243 us
  blocking collectives  124 us (51%)
  starting transfers between devices  43.2 us (18%)
  matrix products  29.9 us (12%)
  waiting for transfers between devices  26 us (11%)
  between operations  11.3 us (5%)
  other arithmetic  7.49 us (3%)
    psum x3, blocking collectives, paired(): lax.psum((local_inner(vector, vector), local_inner(vector, applied)), ('t...  124 us
    ppermute x8, starting transfers between devices, from_behind(): return lax.ppermute(value, axis, pairs)  24.5 us
    dot_general x4, matrix products, adjoint_image(): jnp.einsum('cwgf,cgrsf->cwgrs', image16, kernels, preferred_element_type=...  22 us
    ppermute x8, waiting for transfers between devices, from_behind(): return lax.ppermute(value, axis, pairs)  21.5 us
    ppermute x3, starting transfers between devices, extended(): before = lax.ppermute(last, axis, up)  14.8 us
  transfers between devices with their start and end apart: 14, of which 11 were waited for; matrix products, arithmetic and copies ran while one was open for 0% of the time, Pallas kernels for 0%

commit v1 on v0

--- a/solution.py
+++ b/solution.py
@@ -96,7 +96,7 @@
 
     def paired(vector, applied):
         return lax.psum(
-            (local_inner(vector, vector), local_inner(vector, applied)), ("tile", "wave")
+            lax.psum((local_inner(vector, vector), local_inner(vector, applied)), "tile"), "wave"
         )
 
     applied = operate(residual)

time: 244 us -> 196 us (0.80)
  blocking collectives: 124 us -> 80.1 us
    psum x3 -> x6, blocking collectives: 124 us -> 80.1 us  [the longest x3 61.1 us: paired(): lax.psum((local_inner(vector, vector), local_inner(vector, applied)), 'ti...]
where the time goes in v1:
time: 196 us; the launch traced here: 195 us
  blocking collectives  80.1 us (41%)
  starting transfers between devices  41.4 us (21%)
  matrix products  29.9 us (15%)
  waiting for transfers between devices  23.6 us (12%)
  between operations  12 us (6%)
  other arithmetic  7.54 us (4%)
    psum x3, blocking collectives, paired(): lax.psum((local_inner(vector, vector), local_inner(vector, applied)), 'ti...  61.1 us
    ppermute x8, starting transfers between devices, from_behind(): return lax.ppermute(value, axis, pairs)  23.3 us
    dot_general x4, matrix products, adjoint_image(): jnp.einsum('cwgf,cgrsf->cwgrs', image16, kernels, preferred_element_type=...  22 us
    ppermute x8, waiting for transfers between devices, from_behind(): return lax.ppermute(value, axis, pairs)  19.1 us
    psum x3, blocking collectives, paired(): lax.psum(lax.psum((local_inner(vector, vector), local_inner(vector, appli...  18.9 us
    ppermute x3, starting transfers between devices, extended(): before = lax.ppermute(last, axis, up)  14.3 us
    ppermute x3, waiting for transfers between devices, extended(): before = lax.ppermute(last, axis, up)  4.51 us
  transfers between devices with their start and end apart: 14, of which 11 were waited for; matrix products, arithmetic and copies ran while one was open for 0% of the time, Pallas kernels for 0%

profile of v1, /device:TPU:0, one launch (start us, length us, event | category | flops | bytes accessed | tf_op | source)
XLA Modules:
  0.0 195.2 jit_solution(3631701467831535632)
XLA Ops:
  2.3 3.7 %fusion.12 = f32[32,32,4,128]{3,1,2,0:T(8,128)S(1)} fusion(bf16[1,32,4,128,128]{4,3,2,1,0:T(8,128)(2,1)} %param.21, bf16[32,32,128,1]{2,1,0,3:T(8,128)(2,1)S(1)} %multiply_bitcast_fusion), kind=kOutput, calls=%fused_computation.12 | convolution fusion | flops 134217728 | bytes 6553600 | tf_op jit(solution)/shard_map/cwgf,cgrsf->cwgrs/dot_general | solution.py:48
  8.4 4.9 %collective-permute-start = (bf16[32,4,128]{2,1,0:T(4,128)(2,1)S(1)}, bf16[32,4,128]{2,1,0:T(4,128)(2,1)S(1)}, u32[]{:S(2)}, u32[]{:S(2)}) collective-permute-start(bf16[32,4,128]{2,1,0:T(4,128)(2,1)S(1)} %get-tuple-element.130), channel_id=1, source_target_pairs={{0,4},{4,8},{8,12},{12,16},{16,20},{20,24},{24,28},{1,5},{5,9},{9,... | collective-permute-start | bytes 98312 | tf_op jit(solution)/shard_map/ppermute | solution.py:15
  14.9 4.2 %collective-permute-done.1 = bf16[32,4,128]{2,1,0:T(4,128)(2,1)S(1)} collective-permute-done((bf16[32,4,128]{2,1,0:T(4,128)(2,1)S(1)}, bf16[32,4,128]{2,1,0:T(4,128)(2,1)S(1)}, u32[]{:S(2)}, u32[]{:S(2)}) %collective-permute-start.1) | collective-permute-done | bytes 32800 | tf_op jit(solution)/shard_map/ppermute | solution.py:15
  20.5 5.0 %collective-permute-start.2 = (bf16[32,4,128]{2,1,0:T(4,128)(2,1)S(1)}, bf16[32,4,128]{2,1,0:T(4,128)(2,1)S(1)}, u32[]{:S(2)}, u32[]{:S(2)}) collective-permute-start(bf16[32,4,128]{2,1,0:T(4,128)(2,1)S(1)} %get-tuple-element.135), channel_id=1, source_target_pairs={{0,4},{4,8},{8,12},{12,16},{16,20},{20,24},{24,28},{1,5},{5,9},{9,... | collective-permute-start | bytes 98312 | tf_op jit(solution)/shard_map/ppermute | solution.py:25
  25.6 1.6 collective-permute-done.2
  27.6 6.0 %fusion.8 = f32[32,32,4,128]{3,1,2,0:T(8,128)S(1)} fusion(bf16[1,32,4,128,128]{4,3,2,1,0:T(8,128)(2,1)} %param.21, bf16[32,32,4,128]{3,1,2,0:T(8,128)(2,1)S(1)} %fusion.18, f32[32]{0:T(128)S(1)} %compare_convert_fusion), kind=kOutput, calls=%fused_computation.8 | convolution fusion | flops 268697600 | bytes 7340160 | tf_op jit(solution)/shard_map/cwgf,cgrsf->cwgrs/dot_general | solution.py:48
  35.6 4.8 %collective-permute-start.4 = (bf16[32,4,128]{2,1,0:T(4,128)(2,1)S(1)}, bf16[32,4,128]{2,1,0:T(4,128)(2,1)S(1)}, u32[]{:S(2)}, u32[]{:S(2)}) collective-permute-start(bf16[32,4,128]{2,1,0:T(4,128)(2,1)S(1)} %get-tuple-element.128), channel_id=1, source_target_pairs={{0,4},{4,8},{8,12},{12,16},{16,20},{20,24},{24,28},{1,5},{5,9},{9,... | collective-permute-start | bytes 98312 | tf_op jit(solution)/shard_map/ppermute | solution.py:15
  42.0 5.4 %collective-permute-done.5 = bf16[32,4,128]{2,1,0:T(4,128)(2,1)S(1)} collective-permute-done((bf16[32,4,128]{2,1,0:T(4,128)(2,1)S(1)}, bf16[32,4,128]{2,1,0:T(4,128)(2,1)S(1)}, u32[]{:S(2)}, u32[]{:S(2)}) %collective-permute-start.5) | collective-permute-done | bytes 32800 | tf_op jit(solution)/shard_map/ppermute | solution.py:15
  48.2 20.9 %all-reduce.2 = (f32[]{:T(128)}, f32[]{:T(128)}) all-reduce(f32[]{:T(128)} %get-tuple-element.103, f32[]{:T(128)} %get-tuple-element.102), channel_id=1, replica_groups=mesh['tile'=8,'wave'=4] {'tile'}, use_global_device_ids=true, to_apply=%region_1.0 | all-reduce | flops 2 | bytes 16 | tf_op jit(solution)/shard_map/psum | solution.py:99
  69.0 6.3 %all-reduce.5 = (f32[]{:T(128)}, f32[]{:T(128)}) all-reduce(f32[]{:T(128)} %get-tuple-element.108, f32[]{:T(128)} %get-tuple-element.109), channel_id=1, replica_groups=mesh['tile'=8,'wave'=4] {'wave'}, use_global_device_ids=true, to_apply=%region_2.0 | all-reduce | flops 2 | bytes 16 | tf_op jit(solution)/shard_map/psum | solution.py:98
  78.1 4.7 %collective-permute-start.6 = (bf16[32,4,128]{2,1,0:T(4,128)(2,1)S(1)}, bf16[32,4,128]{2,1,0:T(4,128)(2,1)S(1)}, u32[]{:S(2)}, u32[]{:S(2)}) collective-permute-start(bf16[32,4,128]{2,1,0:T(4,128)(2,1)S(1)} %get-tuple-element.133), channel_id=1, source_target_pairs={{0,4},{4,8},{8,12},{12,16},{16,20},{20,24},{24,28},{1,5},{5,9},{9,... | collective-permute-start | bytes 98312 | tf_op jit(solution)/shard_map/ppermute | solution.py:25
  84.2 1.5 fusion.19
  85.6 6.3 %fusion.4 = f32[32,32,4,128]{3,1,2,0:T(8,128)S(1)} fusion(bf16[1,32,4,128,128]{4,3,2,1,0:T(8,128)(2,1)} %param.21, bf16[32,32,4,128]{3,1,2,0:T(8,128)(2,1)} %fusion.19, f32[32]{0:T(128)S(1)} %compare_convert_fusion), kind=kOutput, calls=%fused_computation.4 | convolution fusion | flops 268697600 | bytes 7340160 | tf_op jit(solution)/shard_map/cwgf,cgrsf->cwgrs/dot_general | solution.py:48
  93.9 4.2 %collective-permute-start.8 = (bf16[32,4,128]{2,1,0:T(4,128)(2,1)S(1)}, bf16[32,4,128]{2,1,0:T(4,128)(2,1)S(1)}, u32[]{:S(2)}, u32[]{:S(2)}) collective-permute-start(bf16[32,4,128]{2,1,0:T(4,128)(2,1)S(1)} %get-tuple-element.126), channel_id=1, source_target_pairs={{0,4},{4,8},{8,12},{12,16},{16,20},{20,24},{24,28},{1,5},{5,9},{9,... | collective-permute-start | bytes 98312 | tf_op jit(solution)/shard_map/ppermute | solution.py:15
  99.7 4.2 %collective-permute-done.9 = bf16[32,4,128]{2,1,0:T(4,128)(2,1)S(1)} collective-permute-done((bf16[32,4,128]{2,1,0:T(4,128)(2,1)S(1)}, bf16[32,4,128]{2,1,0:T(4,128)(2,1)S(1)}, u32[]{:S(2)}, u32[]{:S(2)}) %collective-permute-start.9) | collective-permute-done | bytes 32800 | tf_op jit(solution)/shard_map/ppermute | solution.py:15
  104.7 19.6 %all-reduce.1 = (f32[]{:T(128)}, f32[]{:T(128)}) all-reduce(f32[]{:T(128)} %get-tuple-element.101, f32[]{:T(128)} %get-tuple-element.100), channel_id=1, replica_groups=mesh['tile'=8,'wave'=4] {'tile'}, use_global_device_ids=true, to_apply=%region_7.0 | all-reduce | flops 2 | bytes 16 | tf_op jit(solution)/shard_map/psum | solution.py:99
  124.4 6.3 %all-reduce.4 = (f32[]{:T(128)}, f32[]{:T(128)}) all-reduce(f32[]{:T(128)} %get-tuple-element.106, f32[]{:T(128)} %get-tuple-element.107), channel_id=1, replica_groups=mesh['tile'=8,'wave'=4] {'wave'}, use_global_device_ids=true, to_apply=%region_8.0 | all-reduce | flops 2 | bytes 16 | tf_op jit(solution)/shard_map/psum | solution.py:98
  137.7 4.5 %collective-permute-start.10 = (bf16[32,4,128]{2,1,0:T(4,128)(2,1)S(1)}, bf16[32,4,128]{2,1,0:T(4,128)(2,1)S(1)}, u32[]{:S(2)}, u32[]{:S(2)}) collective-permute-start(bf16[32,4,128]{2,1,0:T(4,128)(2,1)S(1)} %get-tuple-element.131), channel_id=1, source_target_pairs={{0,4},{4,8},{8,12},{12,16},{16,20},{20,24},{24,28},{1,5},{5,9},{9,... | collective-permute-start | bytes 98312 | tf_op jit(solution)/shard_map/ppermute | solution.py:25
  142.2 1.6 collective-permute-done.10
  144.3 6.0 %fusion = f32[32,32,4,128]{3,1,2,0:T(8,128)S(1)} fusion(bf16[1,32,4,128,128]{4,3,2,1,0:T(8,128)(2,1)} %param.21, bf16[32,32,4,128]{3,1,2,0:T(8,128)(2,1)S(1)} %fusion.20, f32[32]{0:T(128)S(1)} %compare_convert_fusion), kind=kOutput, calls=%fused_computation | convolution fusion | flops 268697600 | bytes 7340160 | tf_op jit(solution)/shard_map/cwgf,cgrsf->cwgrs/dot_general | solution.py:48
  152.3 4.2 %collective-permute-start.12 = (bf16[32,4,128]{2,1,0:T(4,128)(2,1)S(1)}, bf16[32,4,128]{2,1,0:T(4,128)(2,1)S(1)}, u32[]{:S(2)}, u32[]{:S(2)}) collective-permute-start(bf16[32,4,128]{2,1,0:T(4,128)(2,1)S(1)} %get-tuple-element.124), channel_id=1, source_target_pairs={{0,4},{4,8},{8,12},{12,16},{16,20},{20,24},{24,28},{1,5},{5,9},{9,... | collective-permute-start | bytes 98312 | tf_op jit(solution)/shard_map/ppermute | solution.py:15
  158.1 4.2 %collective-permute-done.13 = bf16[32,4,128]{2,1,0:T(4,128)(2,1)S(1)} collective-permute-done((bf16[32,4,128]{2,1,0:T(4,128)(2,1)S(1)}, bf16[32,4,128]{2,1,0:T(4,128)(2,1)S(1)}, u32[]{:S(2)}, u32[]{:S(2)}) %collective-permute-start.13) | collective-permute-done | bytes 32800 | tf_op jit(solution)/shard_map/ppermute | solution.py:15
  163.1 20.6 %all-reduce = (f32[]{:T(128)}, f32[]{:T(128)}) all-reduce(f32[]{:T(128)} %get-tuple-element.99, f32[]{:T(128)} %get-tuple-element.98), channel_id=1, replica_groups=mesh['tile'=8,'wave'=4] {'tile'}, use_global_device_ids=true, to_apply=%region_13.0 | all-reduce | flops 2 | bytes 16 | tf_op jit(solution)/shard_map/psum | solution.py:99
  183.8 6.3 %all-reduce.3 = (f32[]{:T(128)}, f32[]{:T(128)}) all-reduce(f32[]{:T(128)} %get-tuple-element.104, f32[]{:T(128)} %get-tuple-element.105), channel_id=1, replica_groups=mesh['tile'=8,'wave'=4] {'wave'}, use_global_device_ids=true, to_apply=%region_14.0 | all-reduce | flops 2 | bytes 16 | tf_op jit(solution)/shard_map/psum | solution.py:98
  (73 shorter events, 26.1 us)
Async XLA Ops:
  6.4 0.7 copy-start.4
  8.4 6.5 %collective-permute-start = (bf16[32,4,128]{2,1,0:T(4,128)(2,1)S(1)}, bf16[32,4,128]{2,1,0:T(4,128)(2,1)S(1)}, u32[]{:S(2)}, u32[]{:S(2)}) collective-permute-start(bf16[32,4,128]{2,1,0:T(4,128)(2,1)S(1)} %get-tuple-element.130), channel_id=1, source_target_pairs={{0,4},{4,8},{8,12},{12,16},{16,20},{20,24},{24,28},{1,5},{5,9},{9,... | collective-permute-start | bytes 98312 | tf_op jit(solution)/shard_map/ppermute | solution.py:15
  13.3 5.8 %collective-permute-start.1 = (bf16[32,4,128]{2,1,0:T(4,128)(2,1)S(1)}, bf16[32,4,128]{2,1,0:T(4,128)(2,1)S(1)}, u32[]{:S(2)}, u32[]{:S(2)}) collective-permute-start(bf16[32,4,128]{2,1,0:T(4,128)(2,1)S(1)} %get-tuple-element.129), channel_id=1, source_target_pairs={{4,0},{8,4},{12,8},{16,12},{20,16},{24,20},{28,24},{5,1},{9,5},{13... | collective-permute-start | bytes 98312 | tf_op jit(solution)/shard_map/ppermute | solution.py:15
  19.2 6.3 %collective-permute-start.3 = (bf16[32,4,128]{2,1,0:T(4,128)(2,1)S(1)}, bf16[32,4,128]{2,1,0:T(4,128)(2,1)S(1)}, u32[]{:S(2)}, u32[]{:S(2)}) collective-permute-start(bf16[32,4,128]{2,1,0:T(4,128)(2,1)S(1)} %get-tuple-element.136), channel_id=1, source_target_pairs={{4,0},{8,4},{12,8},{16,12},{20,16},{24,20},{28,24},{5,1},{9,5},{13... | collective-permute-start | bytes 98312 | tf_op jit(solution)/shard_map/ppermute | solution.py:26
  20.5 6.6 %collective-permute-start.2 = (bf16[32,4,128]{2,1,0:T(4,128)(2,1)S(1)}, bf16[32,4,128]{2,1,0:T(4,128)(2,1)S(1)}, u32[]{:S(2)}, u32[]{:S(2)}) collective-permute-start(bf16[32,4,128]{2,1,0:T(4,128)(2,1)S(1)} %get-tuple-element.135), channel_id=1, source_target_pairs={{0,4},{4,8},{8,12},{12,16},{16,20},{20,24},{24,28},{1,5},{5,9},{9,... | collective-permute-start | bytes 98312 | tf_op jit(solution)/shard_map/ppermute | solution.py:25
  35.6 6.4 %collective-permute-start.4 = (bf16[32,4,128]{2,1,0:T(4,128)(2,1)S(1)}, bf16[32,4,128]{2,1,0:T(4,128)(2,1)S(1)}, u32[]{:S(2)}, u32[]{:S(2)}) collective-permute-start(bf16[32,4,128]{2,1,0:T(4,128)(2,1)S(1)} %get-tuple-element.128), channel_id=1, source_target_pairs={{0,4},{4,8},{8,12},{12,16},{16,20},{20,24},{24,28},{1,5},{5,9},{9,... | collective-permute-start | bytes 98312 | tf_op jit(solution)/shard_map/ppermute | solution.py:15
  40.4 7.0 %collective-permute-start.5 = (bf16[32,4,128]{2,1,0:T(4,128)(2,1)S(1)}, bf16[32,4,128]{2,1,0:T(4,128)(2,1)S(1)}, u32[]{:S(2)}, u32[]{:S(2)}) collective-permute-start(bf16[32,4,128]{2,1,0:T(4,128)(2,1)S(1)} %get-tuple-element.127), channel_id=1, source_target_pairs={{4,0},{8,4},{12,8},{16,12},{20,16},{24,20},{28,24},{5,1},{9,5},{13... | collective-permute-start | bytes 98312 | tf_op jit(solution)/shard_map/ppermute | solution.py:15
  76.7 58.7 %copy-start = (f32[32,16,128]{2,1,0:T(8,128)}, f32[32,16,128]{2,1,0:T(8,128)S(1)}, u32[]{:S(2)}) copy-start(f32[32,16,128]{2,1,0:T(8,128)S(1)} %get-tuple-element.120) | copy-start | bytes 786436
  76.8 6.0 %collective-permute-start.7 = (bf16[32,4,128]{2,1,0:T(4,128)(2,1)S(1)}, bf16[32,4,128]{2,1,0:T(4,128)(2,1)S(1)}, u32[]{:S(2)}, u32[]{:S(2)}) collective-permute-start(bf16[32,4,128]{2,1,0:T(4,128)(2,1)S(1)} %get-tuple-element.134), channel_id=1, source_target_pairs={{4,0},{8,4},{12,8},{16,12},{20,16},{24,20},{28,24},{5,1},{9,5},{13... | collective-permute-start | bytes 98312 | tf_op jit(solution)/shard_map/ppermute | solution.py:26
  78.1 6.1 %collective-permute-start.6 = (bf16[32,4,128]{2,1,0:T(4,128)(2,1)S(1)}, bf16[32,4,128]{2,1,0:T(4,128)(2,1)S(1)}, u32[]{:S(2)}, u32[]{:S(2)}) collective-permute-start(bf16[32,4,128]{2,1,0:T(4,128)(2,1)S(1)} %get-tuple-element.133), channel_id=1, source_target_pairs={{0,4},{4,8},{8,12},{12,16},{16,20},{20,24},{24,28},{1,5},{5,9},{9,... | collective-permute-start | bytes 98312 | tf_op jit(solution)/shard_map/ppermute | solution.py:25
  93.9 5.8 %collective-permute-start.8 = (bf16[32,4,128]{2,1,0:T(4,128)(2,1)S(1)}, bf16[32,4,128]{2,1,0:T(4,128)(2,1)S(1)}, u32[]{:S(2)}, u32[]{:S(2)}) collective-permute-start(bf16[32,4,128]{2,1,0:T(4,128)(2,1)S(1)} %get-tuple-element.126), channel_id=1, source_target_pairs={{0,4},{4,8},{8,12},{12,16},{16,20},{20,24},{24,28},{1,5},{5,9},{9,... | collective-permute-start | bytes 98312 | tf_op jit(solution)/shard_map/ppermute | solution.py:15
  98.1 5.8 %collective-permute-start.9 = (bf16[32,4,128]{2,1,0:T(4,128)(2,1)S(1)}, bf16[32,4,128]{2,1,0:T(4,128)(2,1)S(1)}, u32[]{:S(2)}, u32[]{:S(2)}) collective-permute-start(bf16[32,4,128]{2,1,0:T(4,128)(2,1)S(1)} %get-tuple-element.125), channel_id=1, source_target_pairs={{4,0},{8,4},{12,8},{16,12},{20,16},{24,20},{28,24},{5,1},{9,5},{13... | collective-permute-start | bytes 98312 | tf_op jit(solution)/shard_map/ppermute | solution.py:15
  136.3 5.9 %collective-permute-start.11 = (bf16[32,4,128]{2,1,0:T(4,128)(2,1)S(1)}, bf16[32,4,128]{2,1,0:T(4,128)(2,1)S(1)}, u32[]{:S(2)}, u32[]{:S(2)}) collective-permute-start(bf16[32,4,128]{2,1,0:T(4,128)(2,1)S(1)} %get-tuple-element.132), channel_id=1, source_target_pairs={{4,0},{8,4},{12,8},{16,12},{20,16},{24,20},{28,24},{5,1},{9,5},{13... | collective-permute-start | bytes 98312 | tf_op jit(solution)/shard_map/ppermute | solution.py:26
  137.7 6.1 %collective-permute-start.10 = (bf16[32,4,128]{2,1,0:T(4,128)(2,1)S(1)}, bf16[32,4,128]{2,1,0:T(4,128)(2,1)S(1)}, u32[]{:S(2)}, u32[]{:S(2)}) collective-permute-start(bf16[32,4,128]{2,1,0:T(4,128)(2,1)S(1)} %get-tuple-element.131), channel_id=1, source_target_pairs={{0,4},{4,8},{8,12},{12,16},{16,20},{20,24},{24,28},{1,5},{5,9},{9,... | collective-permute-start | bytes 98312 | tf_op jit(solution)/shard_map/ppermute | solution.py:25
  150.8 11.5 %copy-start.2 = (f32[32,16,128]{2,1,0:T(8,128)S(1)}, f32[32,16,128]{2,1,0:T(8,128)}, u32[]{:S(2)}) copy-start(f32[32,16,128]{2,1,0:T(8,128)} %get-tuple-element.117) | copy-start | bytes 786436
  151.5 42.8 %copy-start.1 = (f32[32,16,128]{2,1,0:T(8,128)S(1)}, f32[32,16,128]{2,1,0:T(8,128)}, u32[]{:S(2)}) copy-start(f32[32,16,128]{2,1,0:T(8,128)} %copy-done) | copy-start | bytes 786436
  151.5 42.8 %copy-start.3 = (f32[32,16,128]{2,1,0:T(8,128)S(1)}, f32[32,16,128]{2,1,0:T(8,128)}, u32[]{:S(2)}) copy-start(f32[32,16,128]{2,1,0:T(8,128)} %get-tuple-element.118) | copy-start | bytes 786436
  152.3 5.8 %collective-permute-start.12 = (bf16[32,4,128]{2,1,0:T(4,128)(2,1)S(1)}, bf16[32,4,128]{2,1,0:T(4,128)(2,1)S(1)}, u32[]{:S(2)}, u32[]{:S(2)}) collective-permute-start(bf16[32,4,128]{2,1,0:T(4,128)(2,1)S(1)} %get-tuple-element.124), channel_id=1, source_target_pairs={{0,4},{4,8},{8,12},{12,16},{16,20},{20,24},{24,28},{1,5},{5,9},{9,... | collective-permute-start | bytes 98312 | tf_op jit(solution)/shard_map/ppermute | solution.py:15
  156.5 5.8 %collective-permute-start.13 = (bf16[32,4,128]{2,1,0:T(4,128)(2,1)S(1)}, bf16[32,4,128]{2,1,0:T(4,128)(2,1)S(1)}, u32[]{:S(2)}, u32[]{:S(2)}) collective-permute-start(bf16[32,4,128]{2,1,0:T(4,128)(2,1)S(1)} %get-tuple-element.123), channel_id=1, source_target_pairs={{4,0},{8,4},{12,8},{16,12},{20,16},{24,20},{28,24},{5,1},{9,5},{13... | collective-permute-start | bytes 98312 | tf_op jit(solution)/shard_map/ppermute | solution.py:15
